TPU v7x, 32 devices: a whole 2x2x4 slice. The times are simulated.
32 devices in a mesh: ctx: 8 (over z, core), fsdp: 4 (over y, x).
Axes of the slice: x: 2, y: 2, z: 4, core: 2. Of those that a mesh axis runs over, the one named last changes fastest.
Arguments:
- tokens: bfloat16 [4, 1024, 2048], P('fsdp', 'ctx'), may hold values from -6 to 6
- cotangent: bfloat16 [4, 1024, 2048], P('fsdp', 'ctx'), may hold values from -6 to 6
- doc_ids: int32 [4, 1024], P('fsdp'), may hold values from 0 to 3, never falling along the last dimension, each value on 1 to 512 neighbouring positions
- block_order: int32 [16], replicated, may hold values from 0 to 15, each once
- front_weight: bfloat16 [2048, 14336], P(None, 'fsdp'), may hold values from -0.125 to 0.125
- back_weight: bfloat16 [10240, 2048], P(None, 'fsdp'), may hold values from -2 to 2
- front_master: float32 [2048, 14336], P('ctx', 'fsdp'), may hold values from -0.125 to 0.125
- back_master: float32 [10240, 2048], P('ctx', 'fsdp'), may hold values from -0.0625 to 0.0625
- front_first: float32 [2048, 14336], P('ctx', 'fsdp'), may hold values from -64 to 64
- back_first: float32 [10240, 2048], P('ctx', 'fsdp'), may hold values from -64 to 64
- front_second: float32 [2048, 14336], P('ctx', 'fsdp'), may hold values from 100 to 10000
- back_second: float32 [10240, 2048], P('ctx', 'fsdp'), may hold values from 2.048 to 204.8
- vectors: float32 [20480], replicated, may hold values from -2 to 2
- vector_first: float32 [20480], replicated, may hold values from -64 to 64
- vector_second: float32 [20480], replicated, may hold values from 100 to 10000
- learn_rates: float32 [3], replicated, may hold values from 0.02 to 0.2
- adam_step: int32 [1], replicated, may hold values from 1 to 8
Outputs:
- layer_out: bfloat16 [4, 1024, 2048], P('fsdp', 'ctx')
- tokens_grad: bfloat16 [4, 1024, 2048], P('fsdp', 'ctx')
- front_grad: float32 [2048, 14336], P('ctx', 'fsdp')
- back_grad: float32 [10240, 2048], P('ctx', 'fsdp')
- vector_grad: float32 [20480], replicated
- front_new: float32 [2048, 14336], P('ctx', 'fsdp')
- back_new: float32 [10240, 2048], P('ctx', 'fsdp')
- vectors_new: float32 [20480], replicated
- front_first_new: float32 [2048, 14336], P('ctx', 'fsdp')
- back_first_new: float32 [10240, 2048], P('ctx', 'fsdp')
- vector_first_new: float32 [20480], replicated
- front_second_new: float32 [2048, 14336], P('ctx', 'fsdp')
- back_second_new: float32 [10240, 2048], P('ctx', 'fsdp')
- vector_second_new: float32 [20480], replicated
- front_next: bfloat16 [2048, 14336], P(None, 'fsdp')
- back_next: bfloat16 [10240, 2048], P(None, 'fsdp')
Inputs may be any that keep to these rules, and one draw needn't show every extreme that they name: `doc_ids`: within a sequence document numbers never fall; a document has 1 to 512 tokens, and one has exactly 512. `block_order`: A permutation of the block numbers.
All inputs are finite; a program needn't handle non-finite values.
Results may differ from a plain program's by a relative error of at most 0.02.
Values may be sent and summed in bfloat16 or wider, within the bound.
A program may use at most 512 MiB of HBM per device.

v0:
```python
import jax
import jax.numpy as jnp
from jax import lax
from jax.sharding import PartitionSpec as P

D = 2048
HEADS = 32
ROT = 32
HEAD_DIM = 64
IN_COLS = 14336
norm_eps = 1e-05
beta_first = 0.9
beta_second = 0.95
adam_eps = 1e-08
weight_decay = 0.1
masked_score = -1e30


def key_block(amount):
    for candidate in (512, 256, 128):
        return candidate
    return amount


def rotary_tables(positions):
    half_rot = ROT // 2
    frequency = jnp.power(10000.0, -2.0 * jnp.arange(half_rot, dtype=jnp.float32) / ROT)
    angles = positions.astype(jnp.float32)[:, None] * frequency[None, :]
    return (jnp.cos(angles), jnp.sin(angles))


def rotate(values, cosine, sine):
    half_rot = ROT // 2
    lower_half = values[..., :half_rot]
    upper_half = values[..., half_rot:ROT]
    cos_full = cosine[:, None, :]
    sin_full = sine[:, None, :]
    return jnp.concatenate(
        [
            lower_half * cos_full - upper_half * sin_full,
            upper_half * cos_full + lower_half * sin_full,
            values[..., ROT:],
        ],
        axis=-1,
    )


def layer_norm(values, norm_gain, norm_shift):
    row_mean = jnp.mean(values, axis=-1, keepdims=True)
    centered = values - row_mean
    variance = jnp.mean(centered * centered, axis=-1, keepdims=True)
    return centered * lax.rsqrt(variance + norm_eps) * norm_gain + norm_shift


def gelu_tanh(values):
    return jax.nn.gelu(values, approximate=True)


def stored_layout(doc_row, block_order):
    block_count = block_order.shape[0]
    block_tokens = doc_row.shape[0] // block_count
    offsets = jnp.arange(block_tokens, dtype=jnp.int32)
    positions = (block_order[:, None] * block_tokens + offsets[None, :]).reshape(-1)
    segments = jnp.take(doc_row.reshape(block_count, block_tokens), block_order, axis=0).reshape(-1)
    return (positions, segments)


def adam_update(weight, first, second, grad, rate, count_now, decay):
    first_new = beta_first * first + (1.0 - beta_first) * grad
    second_new = beta_second * second + (1.0 - beta_second) * grad * grad
    steps_float = count_now.astype(jnp.float32)
    first_fix = 1.0 - jnp.power(beta_first, steps_float)
    second_fix = 1.0 - jnp.power(beta_second, steps_float)
    change = first_new / first_fix / (jnp.sqrt(second_new / second_fix) + adam_eps) + decay * weight
    return (weight - rate * change, first_new, second_new)


def per_device(
    tokens,
    cotangent,
    doc_ids,
    block_order,
    front_weight,
    back_weight,
    front_master,
    back_master,
    front_first,
    back_first,
    front_second,
    back_second,
    vectors,
    vector_first,
    vector_second,
    learn_rates,
    adam_step,
):
    local_rows = tokens.shape[1]
    score_scale = HEAD_DIM ** (-0.5)
    contract_last = (((1,), (1,)), ((), ()))
    contract_first = (((0,), (0,)), ((), ()))
    bias_front = vectors[:IN_COLS]
    bias_back = vectors[IN_COLS : IN_COLS + D]
    norm_gain = vectors[IN_COLS + D : IN_COLS + 2 * D]
    norm_shift = vectors[IN_COLS + 2 * D :]
    positions_all, segments_all = stored_layout(doc_ids[0], block_order)
    seq_len = positions_all.shape[0]
    first_row = lax.axis_index("ctx") * local_rows
    query_pos = lax.dynamic_slice_in_dim(positions_all, first_row, local_rows)
    query_seg = lax.dynamic_slice_in_dim(segments_all, first_row, local_rows)
    inputs = tokens[0].astype(jnp.float32)
    normed, norm_pull = jax.vjp(layer_norm, inputs, norm_gain, norm_shift)
    normed_low = normed.astype(jnp.bfloat16)
    hidden = (
        jnp.dot(
            normed_low,
            lax.all_gather(front_weight, "fsdp", axis=1, tiled=True),
            preferred_element_type=jnp.float32,
        )
        + bias_front
    )
    cosine, sine = rotary_tables(query_pos)

    def rotate_pair(query_raw, key_raw):
        return (rotate(query_raw, cosine, sine), rotate(key_raw, cosine, sine))

    shaped = (local_rows, HEADS, HEAD_DIM)
    (query_rot, key_rot), rotary_pull = jax.vjp(
        rotate_pair, hidden[:, :D].reshape(shaped), hidden[:, D : 2 * D].reshape(shaped)
    )
    query_low = query_rot.astype(jnp.bfloat16)
    key_low = key_rot.reshape(local_rows, D).astype(jnp.bfloat16)
    value_low = hidden[:, 2 * D : 3 * D].astype(jnp.bfloat16)
    hidden_up = hidden[:, 3 * D :]

    def allowed_pairs(offset, block_len):
        key_pos = lax.dynamic_slice_in_dim(positions_all, offset, block_len)
        key_seg = lax.dynamic_slice_in_dim(segments_all, offset, block_len)
        return (key_pos[None, :] <= query_pos[:, None]) & (key_seg[None, :] == query_seg[:, None])

    start_state = (
        jnp.full((HEADS, local_rows), masked_score, jnp.float32),
        jnp.zeros((HEADS, local_rows), jnp.float32),
        jnp.zeros((HEADS, local_rows, HEAD_DIM), jnp.float32),
    )
    running = start_state
    key_piece = lax.all_gather(key_low, "ctx", axis=0, tiled=True)
    value_piece = lax.all_gather(value_low, "ctx", axis=0, tiled=True)
    amount = key_piece.shape[0]
    block_len = key_block(amount)

    def absorb_one_block(carried, block_number):
        block_start = block_number * block_len
        key_part = lax.dynamic_slice_in_dim(key_piece, block_start, block_len).reshape(
            block_len, HEADS, HEAD_DIM
        )
        value_part = lax.dynamic_slice_in_dim(value_piece, block_start, block_len).reshape(
            block_len, HEADS, HEAD_DIM
        )
        allowed = allowed_pairs(block_start, block_len)
        running_max, running_sum, running_out = carried
        scores = (
            jnp.einsum("qhd,khd->hqk", query_low, key_part, preferred_element_type=jnp.float32)
            * score_scale
        )
        masked = jnp.where(allowed[None], scores, masked_score)
        new_max = jnp.maximum(running_max, jnp.max(masked, axis=-1))
        weights = jnp.where(allowed[None], jnp.exp(masked - new_max[..., None]), 0.0)
        factor = jnp.exp(running_max - new_max)
        running_sum = running_sum * factor + jnp.sum(weights, axis=-1)
        running_out = running_out * factor[..., None] + jnp.einsum(
            "hqk,khd->hqd",
            weights.astype(jnp.bfloat16),
            value_part,
            preferred_element_type=jnp.float32,
        )
        carried = (new_max, running_sum, running_out)
        return (carried, None)

    running, unused = lax.scan(absorb_one_block, running, jnp.arange(amount // block_len))
    final_max, final_sum, final_out = running
    attended = jnp.transpose(final_out / final_sum[..., None], (1, 0, 2))
    log_total = final_max + jnp.log(final_sum)
    attended_low = attended.reshape(local_rows, D).astype(jnp.bfloat16)
    activation, gelu_pull = jax.vjp(gelu_tanh, hidden_up)
    mixed_low = jnp.concatenate([attended_low, activation.astype(jnp.bfloat16)], axis=1)
    projected = jnp.dot(
        mixed_low,
        lax.all_gather(back_weight, "fsdp", axis=1, tiled=True),
        preferred_element_type=jnp.float32,
    )
    layer_out = (inputs + projected + bias_back).astype(jnp.bfloat16)[None]
    grad_low = cotangent[0]
    grad_cols = grad_low
    mixed_grad = lax.dot_general(
        grad_cols,
        lax.all_gather(back_weight, "fsdp", axis=1, tiled=True),
        contract_last,
        preferred_element_type=jnp.float32,
    )
    attended_grad = mixed_grad[:, :D].reshape(shaped).astype(jnp.bfloat16)
    (up_grad,) = gelu_pull(mixed_grad[:, D:])
    row_delta = jnp.sum(attended_grad.astype(jnp.float32) * attended, axis=-1).T
    back_state = (jnp.zeros(shaped, jnp.float32), jnp.zeros((seq_len, 2 * D), jnp.float32))
    running = back_state
    scatter_key_piece = lax.all_gather(key_low, "ctx", axis=0, tiled=True)
    scatter_value_piece = lax.all_gather(value_low, "ctx", axis=0, tiled=True)
    amount = scatter_key_piece.shape[0]
    scatter_block_len = key_block(amount)

    def scatter_one_block(carried, block_number):
        block_start = block_number * scatter_block_len
        key_part = lax.dynamic_slice_in_dim(
            scatter_key_piece, block_start, scatter_block_len
        ).reshape(scatter_block_len, HEADS, HEAD_DIM)
        value_part = lax.dynamic_slice_in_dim(
            scatter_value_piece, block_start, scatter_block_len
        ).reshape(scatter_block_len, HEADS, HEAD_DIM)
        allowed = allowed_pairs(block_start, scatter_block_len)
        query_grad, key_value_grad = carried
        scores = (
            jnp.einsum("qhd,khd->hqk", query_low, key_part, preferred_element_type=jnp.float32)
            * score_scale
        )
        probs = jnp.where(allowed[None], jnp.exp(scores - log_total[..., None]), 0.0)
        value_grad = jnp.einsum(
            "hqk,qhd->khd",
            probs.astype(jnp.bfloat16),
            attended_grad,
            preferred_element_type=jnp.float32,
        )
        prob_grad = jnp.einsum(
            "qhd,khd->hqk", attended_grad, value_part, preferred_element_type=jnp.float32
        )
        score_grad = (probs * (prob_grad - row_delta[..., None])).astype(jnp.bfloat16)
        query_grad = (
            query_grad
            + jnp.einsum("hqk,khd->qhd", score_grad, key_part, preferred_element_type=jnp.float32)
            * score_scale
        )
        key_grad = (
            jnp.einsum("hqk,qhd->khd", score_grad, query_low, preferred_element_type=jnp.float32)
            * score_scale
        )
        block_grads = jnp.concatenate(
            [key_grad.reshape(scatter_block_len, D), value_grad.reshape(scatter_block_len, D)],
            axis=1,
        )
        key_value_grad = lax.dynamic_update_slice_in_dim(
            key_value_grad, block_grads, block_start, 0
        )
        carried = (query_grad, key_value_grad)
        return (carried, None)

    running, unused = lax.scan(scatter_one_block, running, jnp.arange(amount // scatter_block_len))
    query_grad, key_value_all = running
    key_value_own = lax.psum_scatter(
        key_value_all.astype(jnp.bfloat16), "ctx", scatter_dimension=0, tiled=True
    ).astype(jnp.float32)
    query_pre, key_pre = rotary_pull((query_grad, key_value_own[:, :D].reshape(shaped)))
    hidden_grad = jnp.concatenate(
        [
            query_pre.reshape(local_rows, D),
            key_pre.reshape(local_rows, D),
            key_value_own[:, D:],
            up_grad,
        ],
        axis=1,
    ).astype(jnp.bfloat16)
    grad_cols = hidden_grad
    normed_grad = lax.dot_general(
        grad_cols,
        lax.all_gather(front_weight, "fsdp", axis=1, tiled=True),
        contract_last,
        preferred_element_type=jnp.float32,
    )
    input_grad, gain_grad, shift_grad = norm_pull(normed_grad)
    tokens_grad = (grad_low.astype(jnp.float32) + input_grad).astype(jnp.bfloat16)[None]
    front_term = lax.psum_scatter(
        lax.dot_general(
            normed_low, hidden_grad, contract_first, preferred_element_type=jnp.float32
        ).astype(jnp.bfloat16),
        "ctx",
        scatter_dimension=0,
        tiled=True,
    )
    back_term = lax.psum_scatter(
        lax.dot_general(
            mixed_low, grad_low, contract_first, preferred_element_type=jnp.float32
        ).astype(jnp.bfloat16),
        "ctx",
        scatter_dimension=0,
        tiled=True,
    )
    front_grad, back_grad = (
        lax.psum_scatter(front_term, "fsdp", scatter_dimension=1, tiled=True).astype(jnp.float32),
        lax.psum_scatter(back_term, "fsdp", scatter_dimension=1, tiled=True).astype(jnp.float32),
    )
    vector_term = jnp.concatenate(
        [
            jnp.sum(hidden_grad, axis=0, dtype=jnp.float32),
            jnp.sum(grad_low, axis=0, dtype=jnp.float32),
            gain_grad,
            shift_grad,
        ]
    )
    vector_grad = lax.psum(vector_term, ("ctx", "fsdp"))
    count_now = adam_step[0]
    front_new, front_first_new, front_second_new = adam_update(
        front_master, front_first, front_second, front_grad, learn_rates[0], count_now, weight_decay
    )
    back_new, back_first_new, back_second_new = adam_update(
        back_master, back_first, back_second, back_grad, learn_rates[1], count_now, weight_decay
    )
    vectors_new, vector_first_new, vector_second_new = adam_update(
        vectors, vector_first, vector_second, vector_grad, learn_rates[2], count_now, 0.0
    )
    front_next, back_next = (
        lax.all_gather(front_new.astype(jnp.bfloat16), "ctx", axis=0, tiled=True),
        lax.all_gather(back_new.astype(jnp.bfloat16), "ctx", axis=0, tiled=True),
    )
    return (
        layer_out,
        tokens_grad,
        front_grad,
        back_grad,
        vector_grad,
        front_new,
        back_new,
        vectors_new,
        front_first_new,
        back_first_new,
        vector_first_new,
        front_second_new,
        back_second_new,
        vector_second_new,
        front_next,
        back_next,
    )


def solution(mesh):
    in_specs = (
        P("fsdp", "ctx", None),
        P("fsdp", "ctx", None),
        P("fsdp", None),
        P(),
        P(None, "fsdp"),
        P(None, "fsdp"),
        P("ctx", "fsdp"),
        P("ctx", "fsdp"),
        P("ctx", "fsdp"),
        P("ctx", "fsdp"),
        P("ctx", "fsdp"),
        P("ctx", "fsdp"),
        P(),
        P(),
        P(),
        P(),
        P(),
    )
    out_specs = (
        P("fsdp", "ctx", None),
        P("fsdp", "ctx", None),
        P("ctx", "fsdp"),
        P("ctx", "fsdp"),
        P(),
        P("ctx", "fsdp"),
        P("ctx", "fsdp"),
        P(),
        P("ctx", "fsdp"),
        P("ctx", "fsdp"),
        P(),
        P("ctx", "fsdp"),
        P("ctx", "fsdp"),
        P(),
        P(None, "fsdp"),
        P(None, "fsdp"),
    )
    return jax.shard_map(
        per_device, mesh=mesh, in_specs=in_specs, out_specs=out_specs, check_vma=False
    )
```

profile of v0, /device:TPU:0, one launch (start us, length us, event | category | flops | bytes accessed | tf_op | source)
XLA Modules:
  0.0 2660.3 jit_solution(6433679246068548918)
XLA Ops:
  10.5 509.2 %all-gather.7.cloned.1.call-done = bf16[2048,14336]{1,0:T(8,128)(2,1)} async-done(((bf16[2048,3584]{1,0:T(8,128)(2,1)}), bf16[2048,14336]{1,0:T(8,128)(2,1)}) %all-gather.7.cloned.1.call-update) | async-done | bytes 58720272 | tf_op jit(solution)/shard_map/all_gather | solution.py:116
  519.8 31.0 %convolution_add_fusion = f32[128,14336]{1,0:T(8,128)} fusion(bf16[2048,14336]{1,0:T(8,128)(2,1)} %all-gather.7.cloned.1.call-done, f32[14336]{0:T(1024)S(1)} %slice-done, bf16[1,128,2048]{2,1,0:T(8,128)(2,1)S(1)} %copy-done, f32[2048]{0:T(1024)S(1)} %get-tuple-element.415, f32[2048]{0:T(1024)S(1)} %get-tuple-element.416, f32[128]{0:T(128)S(1)} %fusion.56, ...), kind=kOutput, calls=%fused_computation.42 | convolution fusion | flops 7519600640 | bytes 66659328 | tf_op jit(solution)/shard_map/dot_general | solution.py:114
  561.5 327.4 %all-gather.13.cloned.1.call-done = bf16[10240,2048]{1,0:T(8,128)(2,1)} async-done(((bf16[10240,512]{1,0:T(8,128)(2,1)}), bf16[10240,2048]{1,0:T(8,128)(2,1)}) %all-gather.13.cloned.1.call-update) | async-done | bytes 41943056 | tf_op jit(solution)/shard_map/all_gather | solution.py:188
  888.9 21.6 fusion.53
  913.2 24.8 all-gather.11.cloned.1.call-done
  944.4 42.2 %all-gather.9.cloned.1.call-done = bf16[1024,2048]{0,1:T(8,128)(2,1)} async-done(((bf16[128,2048]{0,1:T(8,128)(2,1)}), bf16[1024,2048]{0,1:T(8,128)(2,1)}) %all-gather.9.cloned.1.call-update) | async-done | bytes 4194320 | tf_op jit(solution)/shard_map/all_gather | solution.py:146
  986.7 22.1 while.28
  1013.5 54.8 %while.29 = (s32[]{:T(128)}, f32[128,32,64]{0,2,1:T(8,128)S(1)}, bf16[1024,4096]{1,0:T(8,128)(2,1)}, s32[2]{0:T(128)S(1)}, bf16[1024,2048]{0,1:T(8,128)(2,1)}, /...) while((s32[]{:T(128)}, f32[128,32,64]{0,2,1:T(8,128)S(1)}, ...), condition=%wide.region_8.9_spmd.clone, body=%wide.region_7.8_spmd.clone.sunk | while | flops 1374617600 | bytes 86242552 | solution.py:254
  1068.3 6.7 fusion.31
  1077.2 18.6 convolution_convert_fusion.1
  1096.0 60.2 %reduce-scatter.8.cloned.1.call-done = bf16[128,4096]{1,0:T(8,128)(2,1)} async-done(((bf16[1024,4096]{1,0:T(8,128)(2,1)}), bf16[128,4096]{1,0:T(8,128)(2,1)}) %reduce-scatter.8.cloned.1.call-update) | async-done | bytes 1048592 | tf_op jit(solution)/shard_map/reduce_scatter | solution.py:256
  1164.4 24.0 convolution_convert_fusion
  1188.5 372.6 %reduce-scatter.16.cloned.1.call-done = bf16[1280,2048]{1,0:T(8,128)(2,1)} async-done(((bf16[10240,2048]{1,0:T(8,128)(2,1)}), bf16[1280,2048]{1,0:T(8,128)(2,1)}) %reduce-scatter.16.cloned.1.call-update) | async-done | bytes 5242896
  1561.2 562.6 %reduce-scatter.10.cloned.1.call-done = bf16[256,14336]{1,0:T(8,128)(2,1)} async-done(((bf16[2048,14336]{1,0:T(8,128)(2,1)}), bf16[256,14336]{1,0:T(8,128)(2,1)}) %reduce-scatter.10.cloned.1.call-update) | async-done | bytes 7340048 | tf_op jit(solution)/shard_map/reduce_scatter | solution.py:278
  2125.3 27.8 %fusion.48 = (f32[128]{0:T(128)S(1)}, f32[128,2048]{1,0:T(8,128)}) fusion(bf16[1,128,2048]{2,1,0:T(8,128)(2,1)S(1)} %copy-done.1, f32[2048]{0:T(1024)S(1)} %copy-done.14, f32[128]{0:T(128)S(1)} %copy-done.20, bf16[2048,14336]{1,0:T(8,128)(2,1)} %all-gather.7.cloned.1.call-done, bf16[128,8192]{1,0:T(8,128)(2,1)S(1)} %copy-done.3, ...), kind=kOutput, calls=%fused_computation.84 | convolution fusion | flops 7532183552 | bytes 63972352 | tf_op jit(solution)/shard_map/dot_general | solution.py:270
  2159.1 27.5 %reduce-scatter.14.cloned.1.call-done = bf16[1280,512]{1,0:T(8,128)(2,1)} async-done(((bf16[1280,2048]{1,0:T(8,128)(2,1)}), bf16[1280,512]{1,0:T(8,128)(2,1)}) %reduce-scatter.14.cloned.1.call-update) | async-done | bytes 1310736 | tf_op jit(solution)/shard_map/reduce_scatter | solution.py:296
  2186.6 8.3 fusion.63
  2195.0 73.3 %reduce-scatter.12.cloned.1.call-done = bf16[256,3584]{1,0:T(8,128)(2,1)} async-done(((bf16[256,14336]{1,0:T(8,128)(2,1)}), bf16[256,3584]{1,0:T(8,128)(2,1)}) %reduce-scatter.12.cloned.1.call-update) | async-done | bytes 1835024 | tf_op jit(solution)/shard_map/reduce_scatter | solution.py:295
  2268.4 10.9 fusion.65
  2279.3 16.8 fusion.36
  2296.1 99.7 %all-reduce.9.cloned.1.call-done = f32[20480]{0:T(1024)} async-done(((f32[20480]{0:T(1024)}), f32[20480]{0:T(1024)}) %all-reduce.9.cloned.1.call-update) | async-done | bytes 81936 | tf_op jit(solution)/shard_map/psum | solution.py:306
  2398.1 101.5 %all-gather.17.cloned.1.call-done = bf16[10240,512]{1,0:T(8,128)(2,1)} async-done(((bf16[1280,512]{1,0:T(8,128)(2,1)}), bf16[10240,512]{1,0:T(8,128)(2,1)}) %all-gather.17.cloned.1.call-update) | async-done | bytes 10485776 | tf_op jit(solution)/shard_map/all_gather | solution.py:319
  2499.6 134.3 %all-gather.15.cloned.1.call-done = bf16[2048,3584]{1,0:T(8,128)(2,1)} async-done(((bf16[256,3584]{1,0:T(8,128)(2,1)}), bf16[2048,3584]{1,0:T(8,128)(2,1)}) %all-gather.15.cloned.1.call-update) | async-done | bytes 14680080 | tf_op jit(solution)/shard_map/all_gather | solution.py:318
  2635.4 13.7 copy.134
  (205 shorter events, 126.5 us)
Async XLA Ops:
  7.2 512.6 %all-gather.7.cloned.1.call-start = ((), (), s32[]{:S(2)}) async-start(), calls=%async_computation.5 | async-start | bytes 73400320 | tf_op jit(solution)/shard_map/all_gather | solution.py:116
  7.9 511.8 %slice-start = ((f32[20480]{0:T(1024)}), f32[14336]{0:T(1024)S(1)}, s32[]{:S(2)}) async-start(f32[20480]{0:T(1024)} %param.33), calls=%async_computation.17 | async-start | bytes 114688 | tf_op jit(solution)/shard_map/slice | solution.py:101
  7.9 881.0 %all-gather.13.cloned.1.call-start = ((), (), s32[]{:S(2)}) async-start(), calls=%async_computation.8 | async-start | bytes 52428800 | tf_op jit(solution)/shard_map/all_gather | solution.py:188
  8.7 929.3 %all-gather.11.cloned.1.call-start = ((), (), s32[]{:S(2)}) async-start(), calls=%async_computation.7 | async-start | bytes 4718592 | tf_op jit(solution)/shard_map/all_gather | solution.py:147
  9.1 541.7 %copy-start.19 = (f32[128]{0:T(128)}, f32[128]{0:T(128)S(1)}, u32[]{:S(2)}) copy-start(f32[128]{0:T(128)S(1)} %broadcast_multiply_fusion) | copy-start | bytes 1540
  9.9 540.9 %copy-start.21 = (f32[128]{0:T(128)}, f32[128]{0:T(128)S(1)}, u32[]{:S(2)}) copy-start(f32[128]{0:T(128)S(1)} %fusion.56) | copy-start | bytes 1540
  10.5 540.2 %copy-start.13 = (f32[2048]{0:T(1024)}, f32[2048]{0:T(1024)S(1)}, u32[]{:S(2)}) copy-start(f32[2048]{0:T(1024)S(1)} %get-tuple-element.416) | copy-start | bytes 24580
  10.5 540.3 %copy-start.15 = (f32[2048]{0:T(1024)}, f32[2048]{0:T(1024)S(1)}, u32[]{:S(2)}) copy-start(f32[2048]{0:T(1024)S(1)} %get-tuple-element.415) | copy-start | bytes 24580
  553.0 433.7 %all-gather.9.cloned.1.call-start = ((), (), s32[]{:S(2)}) async-start(), calls=%async_computation.6 | async-start | bytes 4718592 | tf_op jit(solution)/shard_map/all_gather | solution.py:146
  555.2 333.7 %copy-start.5 = (bf16[1,128,2048]{2,1,0:T(8,128)(2,1)S(1)}, bf16[1,128,2048]{2,1,0:T(8,128)(2,1)}, u32[]{:S(2)}) copy-start(bf16[1,128,2048]{2,1,0:T(8,128)(2,1)} %param.22) | copy-start | bytes 1572868
  559.0 597.1 %reduce-scatter.8.cloned.1.call-start = ((), (), s32[]{:S(2)}) async-start(), calls=%async_computation.9 | async-start | bytes 9437184 | tf_op jit(solution)/shard_map/reduce_scatter | solution.py:256
  1068.3 492.8 %reduce-scatter.16.cloned.1.call-start = ((), (), s32[]{:S(2)}) async-start(), calls=%async_computation.16 | async-start | bytes 47185920
  1095.8 66.5 %copy-start.26 = (f32[128,16]{0,1:T(8,128)S(1)}, f32[128,16]{0,1:T(8,128)}, u32[]{:S(2)}) copy-start(f32[128,16]{0,1:T(8,128)} %copy-done.25) | copy-start | bytes 24580
  1095.9 1027.9 %reduce-scatter.10.cloned.1.call-start = ((), (), s32[]{:S(2)}) async-start(), calls=%async_computation.10 | async-start | bytes 66060288 | tf_op jit(solution)/shard_map/reduce_scatter | solution.py:278
  1188.5 998.2 %reduce-scatter.14.cloned.1.call-start = ((), (), s32[]{:S(2)}) async-start(), calls=%async_computation.12 | async-start | bytes 6553600 | tf_op jit(solution)/shard_map/reduce_scatter | solution.py:296
  1561.2 563.4 %copy-start.30 = (f32[3]{0:T(128)S(1)}, f32[3]{0:T(128)}, u32[]{:S(2)}) copy-start(f32[3]{0:T(128)} %param.36) | copy-start | bytes 40
  1561.2 564.1 %copy-start.3 = (bf16[128,8192]{1,0:T(8,128)(2,1)S(1)}, bf16[128,8192]{1,0:T(8,128)(2,1)}, u32[]{:S(2)}) copy-start(bf16[128,8192]{1,0:T(8,128)(2,1)} %get-tuple-element.398) | copy-start | bytes 6291460
  1561.2 707.2 %reduce-scatter.12.cloned.1.call-start = ((), (), s32[]{:S(2)}) async-start(), calls=%async_computation.11 | async-start | bytes 9175040 | tf_op jit(solution)/shard_map/reduce_scatter | solution.py:295
  2123.8 272.0 %all-reduce.9.cloned.1.call-start = ((), (), s32[]{:S(2)}) async-start(), calls=%async_computation.13 | async-start | bytes 163840 | tf_op jit(solution)/shard_map/psum | solution.py:306
  2159.1 340.5 %all-gather.17.cloned.1.call-start = ((), (), s32[]{:S(2)}) async-start(), calls=%async_computation.15 | async-start | bytes 11796480 | tf_op jit(solution)/shard_map/all_gather | solution.py:319
  2195.0 438.9 %all-gather.15.cloned.1.call-start = ((), (), s32[]{:S(2)}) async-start(), calls=%async_computation.14 | async-start | bytes 16515072 | tf_op jit(solution)/shard_map/all_gather | solution.py:318
  2279.3 116.5 %copy-start.18 = (f32[20480]{0:T(1024)S(1)}, f32[20480]{0:T(1024)}, u32[]{:S(2)}) copy-start(f32[20480]{0:T(1024)} %param.33) | copy-start | bytes 245764
  2279.3 116.5 %copy-start.23 = (f32[20480]{0:T(1024)S(1)}, f32[20480]{0:T(1024)}, u32[]{:S(2)}) copy-start(f32[20480]{0:T(1024)} %param.35) | copy-start | bytes 245764
  2279.3 116.5 %copy-start.24 = (f32[20480]{0:T(1024)S(1)}, f32[20480]{0:T(1024)}, u32[]{:S(2)}) copy-start(f32[20480]{0:T(1024)} %param.34) | copy-start | bytes 245764
  (24 other events, 271.8 us)
Sparse Core Ops, SparseCore 0:
  9.8 509.8 all-gather.6
  521.6 367.2 all-gather.12
  891.1 46.8 all-gather.10
  940.0 46.5 all-gather.8
  1068.4 87.6 reduce-scatter.7
  1158.4 402.7 reduce-scatter.15
  1563.5 560.2 reduce-scatter.9
  2126.8 59.8 reduce-scatter.13
  2189.6 78.7 reduce-scatter.11
  2274.4 121.3 all-reduce.8
  2398.1 101.4 all-gather.16
  2501.6 132.2 all-gather.14
where the time goes:
time: 2670 us; the launch traced here: 2660 us
  waiting for transfers between devices  2340 us (88%)
  matrix products  169 us (6%)
  local copies, waits for them, and re-layouts  82.6 us (3%)
  other arithmetic  52.3 us (2%)
    reduce_scatter x1, waiting for transfers between devices, per_device(): lax.psum_scatter(lax.dot_general(normed_low, hidden_grad, contract_first,...  563 us
    all_gather x1, waiting for transfers between devices, per_device(): lax.all_gather(front_weight, 'fsdp', axis=1, tiled=True)  509 us
    unnamed x13, waiting for transfers between devices  374 us
    all_gather x1, waiting for transfers between devices, per_device(): lax.all_gather(back_weight, 'fsdp', axis=1, tiled=True)  327 us
    all_gather x1, waiting for transfers between devices, per_device(): lax.all_gather(front_new.astype(jnp.bfloat16), 'ctx', axis=0, tiled=True)  134 us
    all_gather x1, waiting for transfers between devices, per_device(): lax.all_gather(back_new.astype(jnp.bfloat16), 'ctx', axis=0, tiled=True)  102 us
    psum x1, waiting for transfers between devices, per_device(): vector_grad = lax.psum(vector_term, ('ctx', 'fsdp'))  99.7 us
    reduce_scatter x1, waiting for transfers between devices, per_device(): lax.psum_scatter(front_term, 'fsdp', scatter_dimension=1, tiled=True)  73.3 us
  transfers between devices with their start and end apart: 12, of which 12 were waited for; matrix products, arithmetic and copies ran while one was open for 8% of the time, Pallas kernels for 0%

commit v1 on v0

--- a/solution.py
+++ b/solution.py
@@ -143,8 +143,11 @@
         jnp.zeros((HEADS, local_rows, HEAD_DIM), jnp.float32),
     )
     running = start_state
-    key_piece = lax.all_gather(key_low, "ctx", axis=0, tiled=True)
-    value_piece = lax.all_gather(value_low, "ctx", axis=0, tiled=True)
+    key_piece, value_piece = jnp.split(
+        lax.all_gather(jnp.concatenate([key_low, value_low], axis=1), "ctx", axis=0, tiled=True),
+        [key_low.shape[1]],
+        axis=1,
+    )
     amount = key_piece.shape[0]
     block_len = key_block(amount)
 

time: 2670 us -> 2770 us (1.037)
  matrix products: 169 us -> 218 us
  local copies, waits for them, and re-layouts: 82.6 us -> 111 us
    all_gather x2 -> x3, waiting for transfers between devices: 67 us -> 83.6 us  [the longest x1 59 us: per_device(): lax.all_gather(jnp.concatenate([key_low, value_low], axis=1), 'ctx', axis...]
    unnamed x13 -> x14, waiting for transfers between devices: 374 us -> 372 us
  transfers between devices with their start and end apart: 12 -> 13, of which waited for: 12 -> 12; matrix products, arithmetic and copies ran while one was open for 8% -> 10% of each run, Pallas kernels for 0% -> 0%
where the time goes in v1:
time: 2770 us; the launch traced here: 2760 us
  waiting for transfers between devices  2350 us (85%)
  matrix products  218 us (8%)
  local copies, waits for them, and re-layouts  111 us (4%)
  other arithmetic  61.6 us (2%)
    reduce_scatter x1, waiting for transfers between devices, per_device(): lax.psum_scatter(lax.dot_general(normed_low, hidden_grad, contract_first,...  563 us
    all_gather x1, waiting for transfers between devices, per_device(): lax.all_gather(front_weight, 'fsdp', axis=1, tiled=True)  509 us
    unnamed x14, waiting for transfers between devices  372 us
    all_gather x1, waiting for transfers between devices, per_device(): lax.all_gather(back_weight, 'fsdp', axis=1, tiled=True)  326 us
    all_gather x1, waiting for transfers between devices, per_device(): lax.all_gather(front_new.astype(jnp.bfloat16), 'ctx', axis=0, tiled=True)  134 us
    all_gather x1, waiting for transfers between devices, per_device(): lax.all_gather(back_new.astype(jnp.bfloat16), 'ctx', axis=0, tiled=True)  101 us
    psum x1, waiting for transfers between devices, per_device(): vector_grad = lax.psum(vector_term, ('ctx', 'fsdp'))  99.4 us
    reduce_scatter x1, waiting for transfers between devices, per_device(): lax.psum_scatter(front_term, 'fsdp', scatter_dimension=1, tiled=True)  73.1 us
  transfers between devices with their start and end apart: 13, of which 12 were waited for; matrix products, arithmetic and copies ran while one was open for 10% of the time, Pallas kernels for 0%

profile of v1, /device:TPU:0, one launch (start us, length us, event | category | flops | bytes accessed | tf_op | source)
XLA Modules:
  0.0 2759.7 jit_solution(5935328656028672768)
XLA Ops:
  10.8 509.0 %all-gather.8.cloned.1.call-done = bf16[2048,14336]{1,0:T(8,128)(2,1)} async-done(((bf16[2048,3584]{1,0:T(8,128)(2,1)}), bf16[2048,14336]{1,0:T(8,128)(2,1)}) %all-gather.8.cloned.1.call-update) | async-done | bytes 58720272 | tf_op jit(solution)/shard_map/all_gather | solution.py:116
  519.8 30.9 %convolution_add_fusion = f32[128,14336]{1,0:T(8,128)} fusion(bf16[2048,14336]{1,0:T(8,128)(2,1)} %all-gather.8.cloned.1.call-done, f32[14336]{0:T(1024)S(1)} %slice-done, bf16[1,128,2048]{2,1,0:T(8,128)(2,1)S(1)} %copy-done.3, f32[2048]{0:T(1024)S(1)} %get-tuple-element.415, f32[2048]{0:T(1024)S(1)} %get-tuple-element.416, f32[128]{0:T(128)S(1)} %fusion.56, ...), kind=kOutput, calls=%fused_computation.42 | convolution fusion | flops 7519600640 | bytes 66659328 | tf_op jit(solution)/shard_map/dot_general | solution.py:114
  562.5 326.4 %all-gather.12.cloned.1.call-done = bf16[10240,2048]{1,0:T(8,128)(2,1)} async-done(((bf16[10240,512]{1,0:T(8,128)(2,1)}), bf16[10240,2048]{1,0:T(8,128)(2,1)}) %all-gather.12.cloned.1.call-update) | async-done | bytes 41943056 | tf_op jit(solution)/shard_map/all_gather | solution.py:191
  888.9 22.0 fusion.53
  914.2 59.0 %all-gather.10.cloned.1.call-done = bf16[1024,4096]{1,0:T(8,128)(2,1)} async-done(((bf16[128,4096]{1,0:T(8,128)(2,1)}), bf16[1024,4096]{1,0:T(8,128)(2,1)}) %all-gather.10.cloned.1.call-update) | async-done | bytes 8388624 | tf_op jit(solution)/shard_map/all_gather | solution.py:147
  979.3 63.2 %while.28 = (s32[]{:T(128)}, f32[32,128]{1,0:T(8,128)S(1)}, f32[32,128]{1,0:T(8,128)S(1)}, f32[32,128,64]{1,2,0:T(8,128)}, s32[2]{0:T(128)S(1)}, /*index=5*/s32[...) while((s32[]{:T(128)}, f32[32,128]{1,0:T(8,128)S(1)}, ...), condition=%wide.region_5.6_spmd.clone, body=%wide.region_2.0_spmd.clone.sunk | while | flops 565137408 | bytes 49296620 | solution.py:182
  1044.1 24.6 all-gather.16.cloned.1.call-done
  1073.1 94.5 %while.29 = (s32[]{:T(128)}, f32[128,32,64]{0,2,1:T(8,128)}, bf16[1024,4096]{1,0:T(8,128)(2,1)}, s32[2]{0:T(128)S(1)}, bf16[1024,2048]{0,1:T(8,128)(2,1)}, /*ind...) while((s32[]{:T(128)}, f32[128,32,64]{0,2,1:T(8,128)}, ...), condition=%wide.region_8.9_spmd.clone, body=%wide.region_7.8_spmd.clone.sunk | while | flops 1374617600 | bytes 123991352 | solution.py:257
  1086.7 9.0 fusion.134
  1133.7 9.0 fusion.134
  1176.5 16.9 convolution_convert_fusion.1
  1195.5 60.5 %reduce-scatter.8.cloned.1.call-done = bf16[128,4096]{1,0:T(8,128)(2,1)} async-done(((bf16[1024,4096]{1,0:T(8,128)(2,1)}), bf16[128,4096]{1,0:T(8,128)(2,1)}) %reduce-scatter.8.cloned.1.call-update) | async-done | bytes 1048592 | tf_op jit(solution)/shard_map/reduce_scatter | solution.py:259
  1267.1 24.1 convolution_convert_fusion
  1291.2 370.0 %reduce-scatter.16.cloned.1.call-done = bf16[1280,2048]{1,0:T(8,128)(2,1)} async-done(((bf16[10240,2048]{1,0:T(8,128)(2,1)}), bf16[1280,2048]{1,0:T(8,128)(2,1)}) %reduce-scatter.16.cloned.1.call-update) | async-done | bytes 5242896
  1661.3 562.6 %reduce-scatter.10.cloned.1.call-done = bf16[256,14336]{1,0:T(8,128)(2,1)} async-done(((bf16[2048,14336]{1,0:T(8,128)(2,1)}), bf16[256,14336]{1,0:T(8,128)(2,1)}) %reduce-scatter.10.cloned.1.call-update) | async-done | bytes 7340048 | tf_op jit(solution)/shard_map/reduce_scatter | solution.py:281
  2225.3 27.6 fusion.48
  2258.8 27.9 %reduce-scatter.14.cloned.1.call-done = bf16[1280,512]{1,0:T(8,128)(2,1)} async-done(((bf16[1280,2048]{1,0:T(8,128)(2,1)}), bf16[1280,512]{1,0:T(8,128)(2,1)}) %reduce-scatter.14.cloned.1.call-update) | async-done | bytes 1310736 | tf_op jit(solution)/shard_map/reduce_scatter | solution.py:299
  2295.1 73.1 %reduce-scatter.12.cloned.1.call-done = bf16[256,3584]{1,0:T(8,128)(2,1)} async-done(((bf16[256,14336]{1,0:T(8,128)(2,1)}), bf16[256,3584]{1,0:T(8,128)(2,1)}) %reduce-scatter.12.cloned.1.call-update) | async-done | bytes 1835024 | tf_op jit(solution)/shard_map/reduce_scatter | solution.py:298
  2368.3 10.7 fusion.65
  2379.1 17.4 fusion.36
  2396.5 99.4 %all-reduce.9.cloned.1.call-done = f32[20480]{0:T(1024)} async-done(((f32[20480]{0:T(1024)}), f32[20480]{0:T(1024)}) %all-reduce.9.cloned.1.call-update) | async-done | bytes 81936 | tf_op jit(solution)/shard_map/psum | solution.py:309
  2498.2 100.8 %all-gather.20.cloned.1.call-done = bf16[10240,512]{1,0:T(8,128)(2,1)} async-done(((bf16[1280,512]{1,0:T(8,128)(2,1)}), bf16[10240,512]{1,0:T(8,128)(2,1)}) %all-gather.20.cloned.1.call-update) | async-done | bytes 10485776 | tf_op jit(solution)/shard_map/all_gather | solution.py:322
  2598.9 134.5 %all-gather.18.cloned.1.call-done = bf16[2048,3584]{1,0:T(8,128)(2,1)} async-done(((bf16[256,3584]{1,0:T(8,128)(2,1)}), bf16[2048,3584]{1,0:T(8,128)(2,1)}) %all-gather.18.cloned.1.call-update) | async-done | bytes 14680080 | tf_op jit(solution)/shard_map/all_gather | solution.py:321
  2734.9 13.7 copy.148
  (224 shorter events, 212.1 us)
Async XLA Ops:
  7.2 512.6 %all-gather.8.cloned.1.call-start = ((), (), s32[]{:S(2)}) async-start(), calls=%async_computation.5 | async-start | bytes 73400320 | tf_op jit(solution)/shard_map/all_gather | solution.py:116
  7.9 511.8 %slice-start = ((f32[20480]{0:T(1024)}), f32[14336]{0:T(1024)S(1)}, s32[]{:S(2)}) async-start(f32[20480]{0:T(1024)} %param.33), calls=%async_computation.18 | async-start | bytes 114688 | tf_op jit(solution)/shard_map/slice | solution.py:101
  8.0 881.0 %all-gather.12.cloned.1.call-start = ((), (), s32[]{:S(2)}) async-start(), calls=%async_computation.7 | async-start | bytes 52428800 | tf_op jit(solution)/shard_map/all_gather | solution.py:191
  8.7 964.5 %all-gather.10.cloned.1.call-start = ((), (), s32[]{:S(2)}) async-start(), calls=%async_computation.6 | async-start | bytes 9437184 | tf_op jit(solution)/shard_map/all_gather | solution.py:147
  9.2 510.6 %copy-start.20 = (f32[128]{0:T(128)}, f32[128]{0:T(128)S(1)}, u32[]{:S(2)}) copy-start(f32[128]{0:T(128)S(1)} %broadcast_multiply_fusion) | copy-start | bytes 1540
  9.5 510.3 %copy-start.22 = (f32[128]{0:T(128)}, f32[128]{0:T(128)S(1)}, u32[]{:S(2)}) copy-start(f32[128]{0:T(128)S(1)} %fusion.56) | copy-start | bytes 1540
  10.1 546.6 %copy-start.26 = (f32[128,16]{0,1:T(8,128)}, f32[128,16]{0,1:T(8,128)S(1)}, u32[]{:S(2)}) copy-start(f32[128,16]{0,1:T(8,128)S(1)} %get-tuple-element.421) | copy-start | bytes 24580
  10.2 546.6 %copy-start.28 = (f32[128,16]{0,1:T(8,128)}, f32[128,16]{0,1:T(8,128)S(1)}, u32[]{:S(2)}) copy-start(f32[128,16]{0,1:T(8,128)S(1)} %get-tuple-element.422) | copy-start | bytes 24580
  10.8 509.0 %copy-start.14 = (f32[2048]{0:T(1024)}, f32[2048]{0:T(1024)S(1)}, u32[]{:S(2)}) copy-start(f32[2048]{0:T(1024)S(1)} %get-tuple-element.416) | copy-start | bytes 24580
  10.8 509.0 %copy-start.16 = (f32[2048]{0:T(1024)}, f32[2048]{0:T(1024)S(1)}, u32[]{:S(2)}) copy-start(f32[2048]{0:T(1024)S(1)} %get-tuple-element.415) | copy-start | bytes 24580
  556.8 332.2 %copy-start.8 = (bf16[1,128,2048]{2,1,0:T(8,128)(2,1)S(1)}, bf16[1,128,2048]{2,1,0:T(8,128)(2,1)}, u32[]{:S(2)}) copy-start(bf16[1,128,2048]{2,1,0:T(8,128)(2,1)} %param.22) | copy-start | bytes 1572868
  559.8 484.3 %all-gather.14.cloned.1.call-start = ((), (), s32[]{:S(2)}) async-start(), calls=%async_computation.8 | async-start | bytes 4718592 | tf_op jit(solution)/shard_map/all_gather | solution.py:208
  560.4 508.3 %all-gather.16.cloned.1.call-start = ((), (), s32[]{:S(2)}) async-start(), calls=%async_computation.9 | async-start | bytes 4718592 | tf_op jit(solution)/shard_map/all_gather | solution.py:209
  913.6 342.5 %reduce-scatter.8.cloned.1.call-start = ((), (), s32[]{:S(2)}) async-start(), calls=%async_computation.10 | async-start | bytes 9437184 | tf_op jit(solution)/shard_map/reduce_scatter | solution.py:259
  1167.6 493.6 %reduce-scatter.16.cloned.1.call-start = ((), (), s32[]{:S(2)}) async-start(), calls=%async_computation.17 | async-start | bytes 47185920
  1193.5 1030.4 %reduce-scatter.10.cloned.1.call-start = ((), (), s32[]{:S(2)}) async-start(), calls=%async_computation.11 | async-start | bytes 66060288 | tf_op jit(solution)/shard_map/reduce_scatter | solution.py:281
  1291.2 995.5 %reduce-scatter.14.cloned.1.call-start = ((), (), s32[]{:S(2)}) async-start(), calls=%async_computation.13 | async-start | bytes 6553600 | tf_op jit(solution)/shard_map/reduce_scatter | solution.py:299
  1661.2 563.5 %copy-start.31 = (f32[3]{0:T(128)S(1)}, f32[3]{0:T(128)}, u32[]{:S(2)}) copy-start(f32[3]{0:T(128)} %param.36) | copy-start | bytes 40
  1661.2 707.1 %reduce-scatter.12.cloned.1.call-start = ((), (), s32[]{:S(2)}) async-start(), calls=%async_computation.12 | async-start | bytes 9175040 | tf_op jit(solution)/shard_map/reduce_scatter | solution.py:298
  2223.9 272.0 %all-reduce.9.cloned.1.call-start = ((), (), s32[]{:S(2)}) async-start(), calls=%async_computation.14 | async-start | bytes 163840 | tf_op jit(solution)/shard_map/psum | solution.py:309
  2258.8 340.2 %all-gather.20.cloned.1.call-start = ((), (), s32[]{:S(2)}) async-start(), calls=%async_computation.16 | async-start | bytes 11796480 | tf_op jit(solution)/shard_map/all_gather | solution.py:322
  2295.1 438.3 %all-gather.18.cloned.1.call-start = ((), (), s32[]{:S(2)}) async-start(), calls=%async_computation.15 | async-start | bytes 16515072 | tf_op jit(solution)/shard_map/all_gather | solution.py:321
  2379.0 116.9 %copy-start.19 = (f32[20480]{0:T(1024)S(1)}, f32[20480]{0:T(1024)}, u32[]{:S(2)}) copy-start(f32[20480]{0:T(1024)} %param.33) | copy-start | bytes 245764
  2379.1 116.9 %copy-start.24 = (f32[20480]{0:T(1024)S(1)}, f32[20480]{0:T(1024)}, u32[]{:S(2)}) copy-start(f32[20480]{0:T(1024)} %param.35) | copy-start | bytes 245764
  (28 other events, 417.0 us)
Sparse Core Ops, SparseCore 0:
  9.9 509.8 all-gather.7
  521.6 367.2 all-gather.11
  891.1 82.0 all-gather.9
  975.2 46.2 all-gather.13
  1023.5 45.0 all-gather.15
  1167.7 88.3 reduce-scatter.7
  1258.4 402.6 reduce-scatter.15
  1663.5 560.2 reduce-scatter.9
  2226.9 59.7 reduce-scatter.13
  2289.5 78.7 reduce-scatter.11
  2374.4 121.4 all-reduce.8
  2497.4 101.4 all-gather.19
  2601.1 132.2 all-gather.17
